TPU v7x, 32 devices: a whole 2x2x4 slice. The times are simulated.
32 devices in a mesh: scan: 16 (over z, y, x), col: 2 (over core).
Axes of the slice: x: 2, y: 2, z: 4, core: 2. Of those that a mesh axis runs over, the one named last changes fastest.
Arguments:
- frames: float32 [256, 128, 2048], P('scan', None, 'col'), may hold values from -6 to 6
- depth_offset: int32 [128], replicated, may hold values from -64 to 64
- band_width: int32 [128], replicated, may hold values from 1 to 8
- edge_level: int32 [128, 2048], P(None, 'col'), may hold values from 1 to 16
Outputs:
- volume: float32 [256, 128, 2048], P('scan', None, 'col')
All inputs are finite; a program needn't handle non-finite values.
Results may differ from a plain program's by a relative error of at most 0.0003.
Values sent between devices are 32-bit elements; how exact they have to be, the bound alone decides.
A program may use at most 128 MiB of HBM per device.

v0:
```python
import functools

import jax
import jax.numpy as jnp
from jax import lax
from jax.experimental import pallas as pl
from jax.experimental.pallas import tpu as pltpu
from jax.sharding import PartitionSpec as P

SWEEPS = 6
DIFFUSE = 6
BAND = 8
STEP_SIZE = 0.24
LEVEL_SCALE = 16.0
LANES = 128
ROWS = 8
LEAD = 4
FAR_LO = DIFFUSE + BAND - 1
FAR_HI = DIFFUSE + 1
LAG = 2
MESH = pl.DeviceIdType.MESH


def sweep_pass(src, dst, dst_from, n_in, n_out, sweeps, inverse, tiles):
    lead = (n_in - n_out) // 2 + 2 * sweeps - 1

    def advance(t, carry):
        held, flux, made = carry
        at = jnp.minimum(t, n_in - 1)
        new_held, new_flux, new_made = [], [], []
        for s, tile in enumerate(tiles):
            fresh = src[at, tile, :]
            for level in range(sweeps):
                k = s * sweeps + level
                b = fresh if level == 0 else made[k - 1]
                a = held[k]
                c = b - a
                cc = c * c if inverse is None else c * c * inverse[s]
                d = 1.0 + cc
                q = pl.reciprocal(d, approx=True)
                f = c * (q * (2.0 - d * q))
                new_made.append(a + STEP_SIZE * (f - flux[k]))
                new_held.append(b)
                new_flux.append(f)
        return tuple(new_held), tuple(new_flux), tuple(new_made)

    def work(t, carry):
        carry = advance(t + lead, carry)
        for s, tile in enumerate(tiles):
            dst[dst_from + t, tile, :] = carry[2][s * sweeps + sweeps - 1]
        return carry

    start = tuple(src[0, tile, :] for tile in tiles for _ in range(sweeps))
    carry = lax.fori_loop(0, lead, advance, (start, start, start))
    lax.fori_loop(0, n_out, work, carry, unroll=2)


def kernel(group, chunks, off_ref, bw_ref, x, edge, out, *scratch):
    wins = scratch[:chunks]
    (raw, made, prof, edge_v, in_send, in_recv, in_own, halo_send, halo_recv,
     far_send, far_recv, out_send, out_recv, out_own, edge_sem) = scratch[chunks:]
    local = x.shape[0]
    rows = x.shape[1] // group
    frames = local * group
    all_frames = frames * LEAD
    own_at = FAR_LO + frames
    me = lax.axis_index("scan")
    k = lax.rem(me, group)
    z = lax.div(me, group)
    tile_count = rows // ROWS
    pair = 2 if tile_count % 2 == 0 else 1

    def rows_of(j):
        return pl.ds(pl.multiple_of(j * rows, ROWS), rows)

    def cols_of(c):
        return pl.ds(c * LANES, LANES)

    def mate(m):
        return z * group + lax.rem(k + m, group)

    inner = jnp.logical_and(z > 0, z < LEAD - 1)
    has = {1: z < LEAD - 1, -1: z > 0, 2: inner, -2: inner}
    gets = {1: z > 0, -1: z < LEAD - 1, 2: z > 1, -2: z < LEAD - 2}

    barrier = pltpu.get_barrier_semaphore()
    for m in range(1, group):
        pl.semaphore_signal(barrier, inc=1, device_id={"scan": mate(m)}, device_id_type=MESH)
    for step in (1, -1):

        @pl.when(has[step])
        def _(step=step):
            pl.semaphore_signal(
                barrier, inc=1, device_id={"scan": me + step * group}, device_id_type=MESH
            )

    count = group - 1
    for step in (1, -1):
        count = count + has[step].astype(jnp.int32)
    pl.semaphore_wait(barrier, count)

    def in_copy(c, m):
        return pltpu.make_async_remote_copy(
            src_ref=x.at[:, rows_of(lax.rem(k + m, group)), cols_of(c)],
            dst_ref=raw.at[c, pl.ds(SWEEPS + k * local, local)],
            send_sem=in_send.at[c, m - 1],
            recv_sem=in_recv.at[c, m - 1],
            device_id={"scan": mate(m)},
            device_id_type=MESH,
        )

    def in_local(c):
        return pltpu.make_async_copy(
            x.at[:, rows_of(k), cols_of(c)],
            raw.at[c, pl.ds(SWEEPS + k * local, local)],
            in_own.at[c],
        )

    def out_copy(c, m):
        return pltpu.make_async_remote_copy(
            src_ref=made.at[c, pl.ds(lax.rem(k + m, group) * local, local)],
            dst_ref=out.at[:, rows_of(k), cols_of(c)],
            send_sem=out_send.at[c, m - 1],
            recv_sem=out_recv.at[c, m - 1],
            device_id={"scan": mate(m)},
            device_id_type=MESH,
        )

    def out_local(c):
        return pltpu.make_async_copy(
            made.at[c, pl.ds(k * local, local)],
            out.at[:, rows_of(k), cols_of(c)],
            out_own.at[c],
        )

    def z_copy(src, dst, sems, c, i, step):
        send, recv = sems
        return pltpu.make_async_remote_copy(
            src_ref=src,
            dst_ref=dst,
            send_sem=send.at[c, i],
            recv_sem=recv.at[c, i],
            device_id={"scan": me + step * group},
            device_id_type=MESH,
        )

    def halo_copies(c):
        sems = (halo_send, halo_recv)
        up = z_copy(raw.at[c, pl.ds(frames, SWEEPS)], raw.at[c, pl.ds(0, SWEEPS)], sems, c, 0, 1)
        down = z_copy(
            raw.at[c, pl.ds(SWEEPS, SWEEPS)],
            raw.at[c, pl.ds(SWEEPS + frames, SWEEPS)], sems, c, 1, -1,
        )
        return ((1, up), (-1, down))

    def near_copies(c, first):
        win, end = wins[c], own_at + frames

        def one(src, dst, count, i, step):
            return z_copy(
                win.at[pl.ds(src, count)], win.at[pl.ds(dst, count)], (far_send, far_recv), c, i, step
            )

        if first:
            return (
                (1, one(end - FAR_LO, own_at - FAR_LO, FAR_LO, 0, 1)),
                (-1, one(own_at, end, FAR_HI, 1, -1)),
            )
        return (
            (1, one(own_at, FAR_LO, frames - FAR_LO, 2, 1)),
            (-1, one(own_at + FAR_HI, end + FAR_HI, frames - FAR_HI, 3, -1)),
        )

    def far_copies(c):
        win, end = wins[c], own_at + frames
        sems = (far_send, far_recv)
        up = z_copy(win.at[pl.ds(own_at - FAR_LO, FAR_LO)], win.at[pl.ds(0, FAR_LO)], sems, c, 4, 1)
        down = z_copy(
            win.at[pl.ds(end, FAR_HI)], win.at[pl.ds(end + frames, FAR_HI)], sems, c, 5, -1
        )
        return ((2, up), (-2, down))

    def start(copies):
        for step, copy in copies:
            pl.when(has[step])(copy.start)

    def wait_recv(copies):
        for step, copy in copies:
            pl.when(gets[step])(copy.wait_recv)

    def wait_send(copies):
        for step, copy in copies:
            pl.when(has[step])(copy.wait_send)

    edge_copy = pltpu.make_async_copy(edge.at[rows_of(k)], edge_v, edge_sem)
    for c in range(chunks):
        in_local(c).start()
        for m in range(1, group):
            in_copy(c, m).start()
    edge_copy.start()

    def arrive(c):
        in_local(c).wait()
        for m in range(1, group):
            in_copy(c, m).wait_recv()
        start(halo_copies(c))

    def smooth(c):
        wait_recv(halo_copies(c))

        @pl.when(z == 0)
        def _():
            for i in range(SWEEPS):
                raw[c, i] = raw[c, 2 * SWEEPS - 1 - i]

        @pl.when(z == LEAD - 1)
        def _():
            for i in range(SWEEPS):
                raw[c, SWEEPS + frames + i] = raw[c, SWEEPS + frames - 1 - i]

        def one(p, _):
            tiles = [pl.ds(pl.multiple_of((p * pair + s) * ROWS, ROWS), ROWS) for s in range(pair)]
            sweep_pass(
                raw.at[c], wins[c], own_at, frames + 2 * SWEEPS, frames, SWEEPS, None, tiles
            )
            return 0

        lax.fori_loop(0, tile_count // pair, one, 0)
        start(near_copies(c, True))
        start(near_copies(c, False))

    def forward(c):
        wait_recv(near_copies(c, True))
        start(far_copies(c))

    def repeat(win, first, count, source):
        def one(i, _):
            win[first + i] = win[source]
            return 0

        lax.fori_loop(0, count, one, 0)

    def depth(c):
        win = wins[c]
        wait_recv(near_copies(c, False))
        wait_recv(far_copies(c))
        pl.when(z == 0)(lambda: repeat(win, 0, own_at, own_at))
        pl.when(z == 1)(lambda: repeat(win, 0, FAR_LO, FAR_LO))
        end = own_at + frames
        pl.when(z == LEAD - 1)(lambda: repeat(win, end, frames + FAR_HI, end - 1))
        pl.when(z == LEAD - 2)(lambda: repeat(win, end + frames, FAR_HI, end + frames - 1))
        sub = lax.broadcasted_iota(jnp.int32, (ROWS, LANES), 0)

        def one_tile(p, _):
            tile = pl.ds(pl.multiple_of(p * ROWS, ROWS), ROWS)
            row0 = k * rows + p * ROWS
            at_b = [own_at - z * frames + 1 - off_ref[row0 + r] for r in range(ROWS)]
            bws = [bw_ref[row0 + r] for r in range(ROWS)]
            at_a = [at_b[r] - bws[r] for r in range(ROWS)]
            widths = jnp.where(sub == 0, bws[0].astype(jnp.float32), 1.0)
            for r in range(1, ROWS):
                widths = jnp.where(sub == r, bws[r].astype(jnp.float32), widths)

            def fill(d, _):
                at = z * frames + d - DIFFUSE
                at = jnp.where(at < 0, -1 - at, at)
                at = jnp.where(at >= all_frames, 2 * all_frames - 1 - at, at)
                a = win[at + at_a[0], tile, :]
                b = win[at + at_b[0], tile, :]
                for r in range(1, ROWS):
                    a = jnp.where(sub == r, win[at + at_a[r], tile, :], a)
                    b = jnp.where(sub == r, win[at + at_b[r], tile, :], b)
                prof[d, tile, :] = (a - b) / widths
                return 0

            lax.fori_loop(0, frames + 2 * DIFFUSE, fill, 0, unroll=4)
            return 0

        lax.fori_loop(0, tile_count, one_tile, 0)

        def one(p, _):
            tiles = [pl.ds(pl.multiple_of((p * pair + s) * ROWS, ROWS), ROWS) for s in range(pair)]
            inverse = []
            for tile in tiles:
                level = edge_v[tile, pl.ds(c * LANES, LANES)].astype(jnp.float32) / LEVEL_SCALE
                inverse.append(1.0 / (level * level))
            sweep_pass(
                prof, made.at[c], 0, frames + 2 * DIFFUSE, frames, DIFFUSE, inverse, tiles
            )
            return 0

        lax.fori_loop(0, tile_count // pair, one, 0)
        out_local(c).start()
        for m in range(1, group):
            out_copy(c, m).start()

    arrive(0)
    for c in range(chunks):
        if c + 1 < chunks:
            arrive(c + 1)
        if c >= 1:
            forward(c - 1)
        smooth(c)
        if c == 0:
            edge_copy.wait()
        if c >= LAG:
            depth(c - LAG)
    for c in range(max(chunks - LAG, 0), chunks):
        if c == chunks - 1:
            forward(c)
        depth(c)
    for c in range(chunks):
        for m in range(1, group):
            in_copy(c, m).wait_send()
        wait_send(halo_copies(c))
        wait_send(near_copies(c, True))
        wait_send(near_copies(c, False))
        wait_send(far_copies(c))
        out_local(c).wait()
        for m in range(1, group):
            out_copy(c, m).wait()


def body(frames, depth_offset, band_width, edge_level):
    group = lax.axis_size("scan") // LEAD
    local, all_rows, cols = frames.shape
    chunks, rows, block = cols // LANES, all_rows // group, local * group
    dma = pltpu.SemaphoreType.DMA
    smem = pl.BlockSpec(memory_space=pltpu.SMEM)
    anywhere = pl.BlockSpec(memory_space=pl.ANY)
    win = pltpu.VMEM((3 * block + FAR_LO + FAR_HI, rows, LANES), jnp.float32)
    return pl.pallas_call(
        functools.partial(kernel, group, chunks),
        out_shape=jax.ShapeDtypeStruct(frames.shape, frames.dtype),
        in_specs=[smem, smem, anywhere, anywhere],
        out_specs=anywhere,
        scratch_shapes=[win] * chunks
        + [
            pltpu.VMEM((chunks, block + 2 * SWEEPS, rows, LANES), jnp.float32),
            pltpu.VMEM((chunks, block, rows, LANES), jnp.float32),
            pltpu.VMEM((block + 2 * DIFFUSE, rows, LANES), jnp.float32),
            pltpu.VMEM((rows, cols), jnp.int32),
            dma((chunks, group - 1)),
            dma((chunks, group - 1)),
            dma((chunks,)),
            dma((chunks, 2)),
            dma((chunks, 2)),
            dma((chunks, 6)),
            dma((chunks, 6)),
            dma((chunks, group - 1)),
            dma((chunks, group - 1)),
            dma((chunks,)),
            dma,
        ],
        compiler_params=pltpu.CompilerParams(
            collective_id=0, has_side_effects=True, vmem_limit_bytes=60 * 1024 * 1024
        ),
    )(depth_offset, band_width, frames, edge_level)


def solution(mesh):
    placed = (P("scan", None, "col"), P(), P(), P(None, "col"))
    return jax.shard_map(
        body, mesh=mesh, in_specs=placed, out_specs=P("scan", None, "col"), check_vma=False
    )
```

profile of v0, /device:TPU:26, one launch (start us, length us, event | category | flops | bytes accessed | tf_op | source)
XLA Modules:
  0.0 298.3 jit_solution(5200620589258197792)
XLA Ops:
  0.0 289.9 %shard_map.46 = f32[16,128,1024]{2,1,0:T(8,128)} custom-call(s32[128]{0:T(128)} %off_ref.1, s32[128]{0:T(128)} %bw_ref.1, f32[16,128,1024]{2,1,0:T(8,128)} %x.1, s32[128,1024]{1,0:T(8,128)} %edge.1), custom_call_target="tpu_custom_call" | custom-call | tf_op jit(solution)/shard_map/pallas_call | solution.py:332
  289.9 8.4 %copy.6 = f32[16,128,1024]{2,1,0:T(8,128)} copy(f32[16,128,1024]{2,1,0:T(8,128)} %shard_map.46) | data formatting | bytes 16777216
where the time goes:
time: 298 us
  Pallas kernels  290 us (97%)
  local copies, waits for them, and re-layouts  8.44 us (3%)
    pallas_call x1, Pallas kernels, body(): pl.pallas_call(functools.partial(kernel, group, chunks), out_shape=jax.Sh...  290 us
    unnamed x1, local copies, waits for them, and re-layouts  8.44 us

commit v1 on v0

v1 whole, which is shorter than its diff:
```python
import functools

import jax
import jax.numpy as jnp
from jax import lax
from jax.experimental import pallas as pl
from jax.experimental.pallas import tpu as pltpu
from jax.sharding import PartitionSpec as P

SWEEPS = 6
DIFFUSE = 6
BAND = 8
STEP_SIZE = 0.24
LEVEL_SCALE = 16.0
LANES = 128
ROWS = 8
LEAD = 4
LAG = 2
SLOTS = 3
UNROLL = 4
LO = DIFFUSE + BAND - 1
MESH = pl.DeviceIdType.MESH
RATE = 1.0 / STEP_SIZE
UNIT = STEP_SIZE**0.5


def after(block):
    least = DIFFUSE + 1
    return least + -(LO + block + least) % ROWS


def lengths(offset, block):
    beyond = -offset + (DIFFUSE + 1 - after(block))
    up = (jnp.maximum(offset, 0) + ROWS - 1) // ROWS
    down = (jnp.maximum(beyond, 0) + ROWS - 1) // ROWS
    return up, down


def sweep_pass(load, store, n_in, n_out, sweeps, streams):
    lead = (n_in - n_out) // 2 + 2 * sweeps - 1

    def advance(t, carry):
        held, flux, made = carry
        at = jnp.minimum(t, n_in - 1)
        new_held, new_flux, new_made = [], [], []
        for s in range(streams):
            fresh = load(at, s)
            for level in range(sweeps):
                k = s * sweeps + level
                b = fresh if level == 0 else made[k - 1]
                a = held[k]
                c = b - a
                d = RATE + c * c
                q = pl.reciprocal(d, approx=True)
                f = c * (q * (2.0 - d * q))
                new_made.append(a + (f - flux[k]))
                new_held.append(b)
                new_flux.append(f)
        return tuple(new_held), tuple(new_flux), tuple(new_made)

    def work(t, carry):
        carry = advance(t + lead, carry)
        for s in range(streams):
            store(t, s, carry[2][s * sweeps + sweeps - 1])
        return carry

    start = tuple(load(0, s) for s in range(streams) for _ in range(sweeps))
    carry = lax.fori_loop(0, lead, advance, (start, start, start))
    lax.fori_loop(0, n_out, work, carry, unroll=UNROLL)


def kernel(group, chunks, room, off_ref, bw_ref, x, edge, out, *scratch):
    from_up = scratch[:chunks]
    from_down = scratch[chunks : 2 * chunks]
    wins = scratch[2 * chunks : 2 * chunks + SLOTS]
    (raw, made, prof, gain, pack_up, pack_down, edge_v, len_up, len_down, next_up, next_down, base_up, base_down,
     slot_up, slot_down, in_send, in_recv, in_own, halo_send, halo_recv, far_send, far_recv, out_send,
     out_recv, out_own, edge_sem) = scratch[2 * chunks + SLOTS :]
    local = x.shape[0]
    rows = x.shape[1] // group
    block = local * group
    hi = after(block)
    own_at = block + LO
    raw_at = LO + SWEEPS
    n_raw = raw.shape[1]
    ext = LO + block + hi
    spans = block // ROWS
    reach = 2 * block + ext
    me = lax.axis_index("scan")
    k = lax.rem(me, group)
    z = lax.div(me, group)
    tile_count = rows // ROWS
    pair = 2 if tile_count % 2 == 0 else 1

    def rows_of(j):
        return pl.ds(pl.multiple_of(j * rows, ROWS), rows)

    def cols_of(c):
        return pl.ds(c * LANES, LANES)

    def mate(m):
        return z * group + lax.rem(k + m, group)

    has = {1: z < LEAD - 1, -1: z > 0}
    gets = {1: z > 0, -1: z < LEAD - 1}

    barrier = pltpu.get_barrier_semaphore()
    for m in range(1, group):
        pl.semaphore_signal(barrier, inc=1, device_id={"scan": mate(m)}, device_id_type=MESH)
    for step in (1, -1):

        @pl.when(has[step])
        def _(step=step):
            pl.semaphore_signal(
                barrier, inc=1, device_id={"scan": me + step * group}, device_id_type=MESH
            )

    count = group - 1
    for step in (1, -1):
        count = count + has[step].astype(jnp.int32)
    pl.semaphore_wait(barrier, count)

    def in_copy(c, m):
        return pltpu.make_async_remote_copy(
            src_ref=x.at[:, rows_of(lax.rem(k + m, group)), cols_of(c)],
            dst_ref=raw.at[c, pl.ds(raw_at + k * local, local)],
            send_sem=in_send.at[c, m - 1],
            recv_sem=in_recv.at[c, m - 1],
            device_id={"scan": mate(m)},
            device_id_type=MESH,
        )

    def in_local(c):
        return pltpu.make_async_copy(
            x.at[:, rows_of(k), cols_of(c)],
            raw.at[c, pl.ds(raw_at + k * local, local)],
            in_own.at[c],
        )

    def out_copy(c, m):
        return pltpu.make_async_remote_copy(
            src_ref=made.at[c, pl.ds(lax.rem(k + m, group) * local, local)],
            dst_ref=out.at[:, rows_of(k), cols_of(c)],
            send_sem=out_send.at[c, m - 1],
            recv_sem=out_recv.at[c, m - 1],
            device_id={"scan": mate(m)},
            device_id_type=MESH,
        )

    def out_local(c):
        return pltpu.make_async_copy(
            made.at[c, pl.ds(k * local, local)],
            out.at[:, rows_of(k), cols_of(c)],
            out_own.at[c],
        )

    def z_copy(src, dst, sems, c, i, step):
        send, recv = sems
        return pltpu.make_async_remote_copy(
            src_ref=src,
            dst_ref=dst,
            send_sem=send.at[c, i],
            recv_sem=recv.at[c, i],
            device_id={"scan": me + step * group},
            device_id_type=MESH,
        )

    def halo_copies(c):
        sems = (halo_send, halo_recv)
        up = z_copy(
            raw.at[c, pl.ds(block, raw_at)], raw.at[c, pl.ds(0, raw_at)], sems, c, 0, 1
        )
        down = z_copy(
            raw.at[c, pl.ds(raw_at, hi + SWEEPS)],
            raw.at[c, pl.ds(raw_at + block, hi + SWEEPS)], sems, c, 1, -1,
        )
        return ((1, up), (-1, down))

    def far_copies(c):
        sems = (far_send, far_recv)
        up = z_copy(
            pack_up.at[c % SLOTS], from_up[c].at[pl.ds(spans, room)], sems, c, 0, 1
        )
        down = z_copy(
            pack_down.at[c % SLOTS], from_down[c].at[pl.ds(0, room)], sems, c, 1, -1
        )
        return ((1, up), (-1, down))

    def start(copies):
        for step, copy in copies:
            pl.when(has[step])(copy.start)

    def wait_recv(copies):
        for step, copy in copies:
            pl.when(gets[step])(copy.wait_recv)

    def wait_send(copies):
        for step, copy in copies:
            pl.when(has[step])(copy.wait_send)

    edge_copy = pltpu.make_async_copy(edge.at[rows_of(k)], edge_v, edge_sem)
    for c in range(chunks):
        for m in range(1, group):
            in_copy(c, m).start()
        in_local(c).start()
    edge_copy.start()

    for lens, nexts, bases in ((len_up, next_up, base_up), (len_down, next_down, base_down)):
        lens[rows] = jnp.int32(1)
        nexts[rows] = jnp.int32(rows)

    def measure(r, base):
        up, down = lengths(off_ref[k * rows + r], block)
        len_up[r], len_down[r] = up, down
        base_up[r], base_down[r] = base[0] + up, base[1]
        return base[0] + up, base[1] + down

    lax.fori_loop(0, rows, measure, (jnp.int32(0), jnp.int32(0)))

    def link(i, _):
        r = rows - 1 - i
        for lens, nexts in ((len_up, next_up), (len_down, next_down)):
            nexts[r] = jnp.where(lens[r + 1] > 0, r + 1, nexts[r + 1])
        return 0

    lax.fori_loop(0, rows, link, 0)

    def assign(j, carry):
        result = []
        lists = ((len_up, next_up, slot_up, own_at + block - LO), (len_down, next_down, slot_down, own_at + hi))
        for i, (lens, nexts, slots, first) in enumerate(lists):
            row, p = carry[2 * i], carry[2 * i + 1]
            n = lens[row]
            frame = first + ROWS * p - (ROWS * n if i == 0 else 0)
            slots[j] = jnp.where(row < rows, row * reach + frame, own_at)
            done = p + 1 >= n
            result.append(jnp.where(done, nexts[row], row))
            result.append(jnp.where(done, 0, p + 1))
        return tuple(result)

    heads = []
    for lens, nexts in ((len_up, next_up), (len_down, next_down)):
        heads.append(jnp.where(lens[0] > 0, 0, nexts[0]))
        heads.append(jnp.int32(0))
    lax.fori_loop(0, room, assign, tuple(heads))

    def arrive(c):
        in_local(c).wait()
        for m in range(1, group):
            in_copy(c, m).wait_recv()
        start(halo_copies(c))

    def across(win, tile, frame):
        return win.at[pl.ds(tile * (ROWS * reach) + frame, ROWS, stride=reach)]

    def smooth(c):
        win = wins[c % SLOTS]
        wait_recv(halo_copies(c))

        @pl.when(z == 0)
        def _():
            for i in range(raw_at):
                raw[c, raw_at - 1 - i] = raw[c, raw_at + i]

        @pl.when(z == LEAD - 1)
        def _():
            for i in range(hi + SWEEPS):
                raw[c, raw_at + block + i] = raw[c, raw_at + block - 1 - i]

        def one(p, _):
            def load(t, s):
                at = pl.ds(pl.multiple_of((p * pair + s) * ROWS, ROWS), ROWS)
                return raw[c, t, at, :] * (1.0 / UNIT)

            def store(t, s, value):
                across(win, p * pair + s, block + t)[...] = value

            sweep_pass(load, store, n_raw, ext, SWEEPS, pair)
            return 0

        lax.fori_loop(0, tile_count // pair, one, 0)

        def repeat(first, number, source):
            values = [across(win, p, source)[...] for p in range(tile_count)]

            def one(i, _):
                for p in range(tile_count):
                    across(win, p, first + i)[...] = values[p]
                return 0

            lax.fori_loop(0, number, one, 0)

        pl.when(z == 0)(lambda: repeat(0, own_at, own_at))
        pl.when(z == LEAD - 1)(lambda: repeat(own_at + block, hi + block, own_at + block - 1))
        if c >= SLOTS:
            wait_send(far_copies(c - SLOTS))

        def pack(j, _):
            for slots, packed in ((slot_up, pack_up), (slot_down, pack_down)):
                packed[c % SLOTS, j] = win[pl.ds(slots[j], ROWS), :]
            return 0

        lax.fori_loop(0, room, pack, 0, unroll=4)
        start(far_copies(c))

    def unpack(win, source, bases, first):
        def one(r, _):
            base = bases[r]
            for m in range(spans):
                to = pl.multiple_of(r * reach + first + ROWS * m, ROWS)
                win[pl.ds(to, ROWS), :] = source[base + m]
            return 0

        lax.fori_loop(0, rows, one, 0)

    def depth(c):
        win = wins[c % SLOTS]
        wait_recv(far_copies(c))
        pl.when(gets[1])(lambda: unpack(win, from_up[c], base_up, 0))
        pl.when(gets[-1])(lambda: unpack(win, from_down[c], base_down, own_at + block + hi))

        for p in range(tile_count):
            tile = pl.ds(p * ROWS, ROWS)
            gain[tile, :] = LEVEL_SCALE / edge_v[tile, pl.ds(c * LANES, LANES)].astype(jnp.float32)

        def fill(r, _):
            width = bw_ref[k * rows + r]
            at_b = r * reach + own_at - DIFFUSE + 1 - off_ref[k * rows + r]
            at_a = at_b - width
            scale = jnp.broadcast_to(gain[pl.ds(r, 1), :], (ROWS, LANES)) / width.astype(jnp.float32)
            for m in range(prof.shape[0] // (rows * ROWS)):
                a = win[pl.ds(at_a + m * ROWS, ROWS), :]
                b = win[pl.ds(at_b + m * ROWS, ROWS), :]
                prof[pl.ds(m * ROWS * rows + r, ROWS, stride=rows), :] = (a - b) * scale
            return 0

        lax.fori_loop(0, rows, fill, 0)

        def bins(d):
            return pl.ds(d * rows, rows)

        @pl.when(z == 0)
        def _():
            for i in range(DIFFUSE):
                prof[bins(DIFFUSE - 1 - i), :] = prof[bins(DIFFUSE + i), :]

        @pl.when(z == LEAD - 1)
        def _():
            for i in range(DIFFUSE):
                prof[bins(DIFFUSE + block + i), :] = prof[bins(DIFFUSE + block - 1 - i), :]

        def one(p, _):
            tiles = [pl.ds(pl.multiple_of((p * pair + s) * ROWS, ROWS), ROWS) for s in range(pair)]
            scales = [
                edge_v[tile, pl.ds(c * LANES, LANES)].astype(jnp.float32) * (UNIT / LEVEL_SCALE) for tile in tiles
            ]

            def load(t, s):
                return prof[pl.ds(pl.multiple_of(t * rows + (p * pair + s) * ROWS, ROWS), ROWS), :]

            def store(t, s, value):
                made[c, t, tiles[s], :] = value * scales[s]

            sweep_pass(load, store, block + 2 * DIFFUSE, block, DIFFUSE, pair)
            return 0

        lax.fori_loop(0, tile_count // pair, one, 0)
        for m in range(1, group):
            out_copy(c, m).start()
        out_local(c).start()

    arrive(0)
    for c in range(chunks):
        if c + 1 < chunks:
            arrive(c + 1)
        smooth(c)
        if c == 0:
            edge_copy.wait()
        if c >= LAG:
            depth(c - LAG)
    for c in range(max(chunks - LAG, 0), chunks):
        depth(c)
    for c in range(chunks):
        for m in range(1, group):
            in_copy(c, m).wait_send()
        wait_send(halo_copies(c))
        if c >= chunks - SLOTS:
            wait_send(far_copies(c))
        out_local(c).wait()
        for m in range(1, group):
            out_copy(c, m).wait()


def body(frames, depth_offset, band_width, edge_level):
    group = lax.axis_size("scan") // LEAD
    local, all_rows, cols = frames.shape
    chunks, rows, block = cols // LANES, all_rows // group, local * group
    hi, spans = after(block), block // ROWS
    bins = -(-(block + 2 * DIFFUSE) // ROWS) * ROWS
    dma = pltpu.SemaphoreType.DMA
    smem = pl.BlockSpec(memory_space=pltpu.SMEM)
    anywhere = pl.BlockSpec(memory_space=pl.ANY)

    def vmem(*shape):
        return pltpu.VMEM(shape, jnp.float32)

    def table(size):
        return pltpu.SMEM((size,), jnp.int32)

    def with_room(room, call):
        arrived = vmem(spans + room, ROWS, LANES)
        packed = vmem(SLOTS, room, ROWS, LANES)
        return pl.pallas_call(
            functools.partial(kernel, group, chunks, room),
            out_shape=jax.ShapeDtypeStruct(frames.shape, frames.dtype),
            in_specs=[smem, smem, anywhere, anywhere],
            out_specs=anywhere,
            scratch_shapes=[arrived] * (2 * chunks)
            + [vmem((3 * block + LO + hi) * rows, LANES)] * SLOTS
            + [
                vmem(chunks, LO + block + hi + 2 * SWEEPS, rows, LANES),
                vmem(chunks, block, rows, LANES),
                vmem(bins * rows, LANES),
                vmem(rows, LANES),
                packed,
                packed,
                pltpu.VMEM((rows, cols), jnp.int32),
            ]
            + [table(rows + 1)] * 6
            + [table(room)] * 2
            + [
                dma((chunks, group - 1)),
                dma((chunks, group - 1)),
                dma((chunks,)),
                dma((chunks, 2)),
                dma((chunks, 2)),
                dma((chunks, 2)),
                dma((chunks, 2)),
                dma((chunks, group - 1)),
                dma((chunks, group - 1)),
                dma((chunks,)),
                dma,
            ],
            compiler_params=pltpu.CompilerParams(
                collective_id=call, has_side_effects=True, vmem_limit_bytes=60 * 1024 * 1024
            ),
        )

    whole = rows * spans
    half = whole // 2
    taken = [jnp.max(jnp.sum(n.reshape(group, rows), 1)) for n in lengths(depth_offset, block)]
    fits = jnp.maximum(*taken) <= half
    return lax.cond(
        fits, with_room(half, 0), with_room(whole, 1), depth_offset, band_width, frames, edge_level
    )


def solution(mesh):
    placed = (P("scan", None, "col"), P(), P(), P(None, "col"))
    return jax.shard_map(
        body, mesh=mesh, in_specs=placed, out_specs=P("scan", None, "col"), check_vma=False
    )
```

time: 298 us -> 204 us (0.68)
  Pallas kernels: 290 us -> 191 us
    pallas_call x1, Pallas kernels: 290 us -> 191 us  [body(): lax.cond(fits, with_room(half, 0), with_room(whole, 1), depth_offset, ban...]
where the time goes in v1:
time: 204 us
  Pallas kernels  191 us (94%)
  local copies, waits for them, and re-layouts  8.61 us (4%)
  other arithmetic  2.26 us (1%)
    pallas_call x1, Pallas kernels, body(): lax.cond(fits, with_room(half, 0), with_room(whole, 1), depth_offset, ban...  191 us
    unnamed x1, local copies, waits for them, and re-layouts  8.44 us

profile of v1, /device:TPU:26, one launch (start us, length us, event | category | flops | bytes accessed | tf_op | source)
XLA Modules:
  0.0 203.6 jit_solution(921061063962059924)
XLA Ops:
  0.0 0.7 and_select_fusion
  0.7 0.1 reshape.7
  0.8 0.1 reduce_sum.19
  0.9 0.7 reduce_max.19
  1.6 0.1 reshape.6
  1.7 0.1 reduce_sum.18
  1.8 0.6 reduce_max.18
  3.8 191.4 %conditional.1 = (f32[16,128,1024]{2,1,0:T(8,128)}) conditional(s32[]{:T(128)} %convert_element_type.3, (s32[128]{0:T(128)}, s32[128]{0:T(128)}, f32[16,128,1024]{2,1,0:T(8,128)}, s32[128,1024]{1,0:T(8,128)}) %tuple.11, (s32[128]{0:T(128)}, s32[128]{0:T(128)}, f32[16,128,1024]{2,1,0:T(8,128)}, s32[128,1024]{1,0:T(8,128)}) %tuple.11), branch_computations={%region_4.5_spmd, %region_5.6_spmd} | conditional | bytes 8 | solution.py:453
  3.8 191.4 %branch_1_fun.1 = f32[16,128,1024]{2,1,0:T(8,128)} custom-call(s32[128]{0:T(128)} %get-tuple-element.28.off_ref, s32[128]{0:T(128)} %get-tuple-element.29.bw_ref, f32[16,128,1024]{2,1,0:T(8,128)} %get-tuple-element.30.x, s32[128,1024]{1,0:T(8,128)} %get-tuple-element.31.edge), custom_call_target="tpu_custom_call" | custom-call | tf_op jit(solution)/shard_map/cond/branch_1_fun/pallas_call | solution.py:453
  195.2 8.4 %copy.10 = f32[16,128,1024]{2,1,0:T(8,128)} copy(f32[16,128,1024]{2,1,0:T(8,128)} %get-tuple-element.32) | data formatting | bytes 16777216

commit v2 on v1

--- a/solution.py
+++ b/solution.py
@@ -15,7 +15,7 @@
 LANES = 128
 ROWS = 8
 LEAD = 4
-LAG = 2
+LAG = 1
 SLOTS = 3
 UNROLL = 4
 LO = DIFFUSE + BAND - 1
@@ -139,7 +139,7 @@
 
     def out_copy(c, m):
         return pltpu.make_async_remote_copy(
-            src_ref=made.at[c, pl.ds(lax.rem(k + m, group) * local, local)],
+            src_ref=made.at[c % SLOTS, pl.ds(lax.rem(k + m, group) * local, local)],
             dst_ref=out.at[:, rows_of(k), cols_of(c)],
             send_sem=out_send.at[c, m - 1],
             recv_sem=out_recv.at[c, m - 1],
@@ -149,7 +149,7 @@
 
     def out_local(c):
         return pltpu.make_async_copy(
-            made.at[c, pl.ds(k * local, local)],
+            made.at[c % SLOTS, pl.ds(k * local, local)],
             out.at[:, rows_of(k), cols_of(c)],
             out_own.at[c],
         )
@@ -359,15 +359,22 @@
                 return prof[pl.ds(pl.multiple_of(t * rows + (p * pair + s) * ROWS, ROWS), ROWS), :]
 
             def store(t, s, value):
-                made[c, t, tiles[s], :] = value * scales[s]
+                made[c % SLOTS, t, tiles[s], :] = value * scales[s]
 
             sweep_pass(load, store, block + 2 * DIFFUSE, block, DIFFUSE, pair)
             return 0
 
+        if c >= SLOTS:
+            sent(c - SLOTS)
         lax.fori_loop(0, tile_count // pair, one, 0)
         for m in range(1, group):
             out_copy(c, m).start()
         out_local(c).start()
+
+    def sent(c):
+        out_local(c).wait()
+        for m in range(1, group):
+            out_copy(c, m).wait_send()
 
     arrive(0)
     for c in range(chunks):
@@ -386,9 +393,10 @@
         wait_send(halo_copies(c))
         if c >= chunks - SLOTS:
             wait_send(far_copies(c))
-        out_local(c).wait()
-        for m in range(1, group):
-            out_copy(c, m).wait()
+        if c >= chunks - SLOTS:
+            sent(c)
+        for m in range(1, group):
+            out_copy(c, m).wait_recv()
 
 
 def body(frames, depth_offset, band_width, edge_level):
@@ -419,7 +427,7 @@
             + [vmem((3 * block + LO + hi) * rows, LANES)] * SLOTS
             + [
                 vmem(chunks, LO + block + hi + 2 * SWEEPS, rows, LANES),
-                vmem(chunks, block, rows, LANES),
+                vmem(SLOTS, block, rows, LANES),
                 vmem(bins * rows, LANES),
                 vmem(rows, LANES),
                 packed,
@@ -442,7 +450,7 @@
                 dma,
             ],
             compiler_params=pltpu.CompilerParams(
-                collective_id=call, has_side_effects=True, vmem_limit_bytes=60 * 1024 * 1024
+                collective_id=call, has_side_effects=True, vmem_limit_bytes=52 * 1024 * 1024
             ),
         )
 

time: 204 us -> 195 us (0.956)
  local copies, waits for them, and re-layouts: 8.61 us -> 3.56 us
  Pallas kernels: 191 us -> 186 us
    pallas_call x1, Pallas kernels: 191 us -> 186 us  [body(): lax.cond(fits, with_room(half, 0), with_room(whole, 1), depth_offset, ban...]
    unnamed x1, local copies, waits for them, and re-layouts: 8.44 us -> 3.4 us
where the time goes in v2:
time: 195 us; the launch traced here: 194 us
  Pallas kernels  186 us (95%)
  local copies, waits for them, and re-layouts  3.56 us (2%)
  other arithmetic  2.26 us (1%)
    pallas_call x1, Pallas kernels, body(): lax.cond(fits, with_room(half, 0), with_room(whole, 1), depth_offset, ban...  186 us

profile of v2, /device:TPU:26, one launch (start us, length us, event | category | flops | bytes accessed | tf_op | source)
XLA Modules:
  0.0 193.5 jit_solution(15009700841898469973)
XLA Ops:
  0.0 0.7 and_select_fusion
  0.7 0.1 reshape.7
  0.8 0.1 reduce_sum.19
  0.9 0.7 reduce_max.19
  1.6 0.1 reshape.6
  1.7 0.1 reduce_sum.18
  1.8 0.6 reduce_max.18
  3.8 186.3 %conditional.1 = (f32[16,128,1024]{2,1,0:T(8,128)S(1)}) conditional(s32[]{:T(128)} %convert_element_type.3, (s32[128]{0:T(128)}, s32[128]{0:T(128)}, f32[16,128,1024]{2,1,0:T(8,128)}, s32[128,1024]{1,0:T(8,128)}) %tuple.11, (s32[128]{0:T(128)}, s32[128]{0:T(128)}, f32[16,128,1024]{2,1,0:T(8,128)}, s32[128,1024]{1,0:T(8,128)}) %tuple.11), branch_computations={%region_4.5_spmd, %region_5.6_spmd} | conditional | bytes 8 | solution.py:461
  3.8 186.3 %branch_1_fun.1 = f32[16,128,1024]{2,1,0:T(8,128)S(1)} custom-call(s32[128]{0:T(128)} %get-tuple-element.28.off_ref, s32[128]{0:T(128)} %get-tuple-element.29.bw_ref, f32[16,128,1024]{2,1,0:T(8,128)} %get-tuple-element.30.x, s32[128,1024]{1,0:T(8,128)} %get-tuple-element.31.edge), custom_call_target="tpu_custom_call" | custom-call | tf_op jit(solution)/shard_map/cond/branch_1_fun/pallas_call | solution.py:461
  190.1 3.4 %copy.10 = f32[16,128,1024]{2,1,0:T(8,128)} copy(f32[16,128,1024]{2,1,0:T(8,128)S(1)} %get-tuple-element.32) | data formatting | bytes 16777216

commit v3 on v2

--- a/solution.py
+++ b/solution.py
@@ -69,13 +69,13 @@
     lax.fori_loop(0, n_out, work, carry, unroll=UNROLL)
 
 
-def kernel(group, chunks, room, off_ref, bw_ref, x, edge, out, *scratch):
+def kernel(group, chunks, room, offsets, widths, x, edge, out, *scratch):
     from_up = scratch[:chunks]
     from_down = scratch[chunks : 2 * chunks]
     wins = scratch[2 * chunks : 2 * chunks + SLOTS]
     (raw, made, prof, gain, pack_up, pack_down, edge_v, len_up, len_down, next_up, next_down, base_up, base_down,
      slot_up, slot_down, in_send, in_recv, in_own, halo_send, halo_recv, far_send, far_recv, out_send,
-     out_recv, out_own, edge_sem) = scratch[2 * chunks + SLOTS :]
+     out_recv, out_own, edge_sem, off_ref, bw_ref, table_sem) = scratch[2 * chunks + SLOTS :]
     local = x.shape[0]
     rows = x.shape[1] // group
     block = local * group
@@ -98,14 +98,24 @@
     def cols_of(c):
         return pl.ds(c * LANES, LANES)
 
+    mates = sorted(range(1, group), key=lambda m: -m.bit_count())
+
+    def partner(m):
+        at, bit = k, 1
+        while bit < group:
+            if m & bit:
+                at = at + bit - 2 * bit * lax.rem(lax.div(k, bit), 2)
+            bit *= 2
+        return at
+
     def mate(m):
-        return z * group + lax.rem(k + m, group)
+        return z * group + partner(m)
 
     has = {1: z < LEAD - 1, -1: z > 0}
     gets = {1: z > 0, -1: z < LEAD - 1}
 
     barrier = pltpu.get_barrier_semaphore()
-    for m in range(1, group):
+    for m in mates:
         pl.semaphore_signal(barrier, inc=1, device_id={"scan": mate(m)}, device_id_type=MESH)
     for step in (1, -1):
 
@@ -122,7 +132,7 @@
 
     def in_copy(c, m):
         return pltpu.make_async_remote_copy(
-            src_ref=x.at[:, rows_of(lax.rem(k + m, group)), cols_of(c)],
+            src_ref=x.at[:, rows_of(partner(m)), cols_of(c)],
             dst_ref=raw.at[c, pl.ds(raw_at + k * local, local)],
             send_sem=in_send.at[c, m - 1],
             recv_sem=in_recv.at[c, m - 1],
@@ -139,7 +149,7 @@
 
     def out_copy(c, m):
         return pltpu.make_async_remote_copy(
-            src_ref=made.at[c % SLOTS, pl.ds(lax.rem(k + m, group) * local, local)],
+            src_ref=made.at[c % SLOTS, pl.ds(partner(m) * local, local)],
             dst_ref=out.at[:, rows_of(k), cols_of(c)],
             send_sem=out_send.at[c, m - 1],
             recv_sem=out_recv.at[c, m - 1],
@@ -200,10 +210,18 @@
 
     edge_copy = pltpu.make_async_copy(edge.at[rows_of(k)], edge_v, edge_sem)
     for c in range(chunks):
-        for m in range(1, group):
+        for m in mates:
             in_copy(c, m).start()
         in_local(c).start()
     edge_copy.start()
+    table_copies = [
+        pltpu.make_async_copy(src, dst, table_sem.at[i])
+        for i, (src, dst) in enumerate(((offsets, off_ref), (widths, bw_ref)))
+    ]
+    for copy in table_copies:
+        copy.start()
+    for copy in table_copies:
+        copy.wait()
 
     for lens, nexts, bases in ((len_up, next_up, base_up), (len_down, next_down, base_down)):
         lens[rows] = jnp.int32(1)
@@ -246,7 +264,7 @@
 
     def arrive(c):
         in_local(c).wait()
-        for m in range(1, group):
+        for m in mates:
             in_copy(c, m).wait_recv()
         start(halo_copies(c))
 
@@ -367,13 +385,13 @@
         if c >= SLOTS:
             sent(c - SLOTS)
         lax.fori_loop(0, tile_count // pair, one, 0)
-        for m in range(1, group):
+        for m in mates:
             out_copy(c, m).start()
         out_local(c).start()
 
     def sent(c):
         out_local(c).wait()
-        for m in range(1, group):
+        for m in mates:
             out_copy(c, m).wait_send()
 
     arrive(0)
@@ -388,14 +406,14 @@
     for c in range(max(chunks - LAG, 0), chunks):
         depth(c)
     for c in range(chunks):
-        for m in range(1, group):
+        for m in mates:
             in_copy(c, m).wait_send()
         wait_send(halo_copies(c))
         if c >= chunks - SLOTS:
             wait_send(far_copies(c))
         if c >= chunks - SLOTS:
             sent(c)
-        for m in range(1, group):
+        for m in mates:
             out_copy(c, m).wait_recv()
 
 
@@ -406,7 +424,6 @@
     hi, spans = after(block), block // ROWS
     bins = -(-(block + 2 * DIFFUSE) // ROWS) * ROWS
     dma = pltpu.SemaphoreType.DMA
-    smem = pl.BlockSpec(memory_space=pltpu.SMEM)
     anywhere = pl.BlockSpec(memory_space=pl.ANY)
 
     def vmem(*shape):
@@ -421,7 +438,7 @@
         return pl.pallas_call(
             functools.partial(kernel, group, chunks, room),
             out_shape=jax.ShapeDtypeStruct(frames.shape, frames.dtype),
-            in_specs=[smem, smem, anywhere, anywhere],
+            in_specs=[anywhere] * 4,
             out_specs=anywhere,
             scratch_shapes=[arrived] * (2 * chunks)
             + [vmem((3 * block + LO + hi) * rows, LANES)] * SLOTS
@@ -448,6 +465,9 @@
                 dma((chunks, group - 1)),
                 dma((chunks,)),
                 dma,
+                table(all_rows),
+                table(all_rows),
+                dma((2,)),
             ],
             compiler_params=pltpu.CompilerParams(
                 collective_id=call, has_side_effects=True, vmem_limit_bytes=52 * 1024 * 1024
@@ -456,8 +476,10 @@
 
     whole = rows * spans
     half = whole // 2
-    taken = [jnp.max(jnp.sum(n.reshape(group, rows), 1)) for n in lengths(depth_offset, block)]
-    fits = jnp.maximum(*taken) <= half
+    up, down = lengths(depth_offset, block)
+    mine = jnp.arange(all_rows)[None] // rows == jnp.arange(group)[:, None]
+    taken = jnp.sum(jnp.where(mine, up + down * (2 * whole), 0), 1)
+    fits = jnp.max(jnp.maximum(lax.rem(taken, 2 * whole), lax.div(taken, 2 * whole))) <= half
     return lax.cond(
         fits, with_room(half, 0), with_room(whole, 1), depth_offset, band_width, frames, edge_level
     )

time: 195 us -> 193 us (0.990)
  no operation moved by 1% of the time
where the time goes in v3:
time: 193 us; the launch traced here: 191 us
  Pallas kernels  186 us (96%)
  local copies, waits for them, and re-layouts  3.4 us (2%)
    pallas_call x1, Pallas kernels, body(): lax.cond(fits, with_room(half, 0), with_room(whole, 1), depth_offset, ban...  186 us

profile of v3, /device:TPU:26, one launch (start us, length us, event | category | flops | bytes accessed | tf_op | source)
XLA Modules:
  0.0 191.2 jit_solution(16683360130172864776)
XLA Ops:
  0.0 0.7 and_select_fusion.2
  0.7 0.1 select_reduce_fusion
  0.8 0.6 fusion.1
  2.1 185.7 %conditional.1 = (f32[16,128,1024]{2,1,0:T(8,128)S(1)}) conditional(s32[]{:T(128)} %convert_element_type.3, (s32[128]{0:T(128)}, s32[128]{0:T(128)}, f32[16,128,1024]{2,1,0:T(8,128)}, s32[128,1024]{1,0:T(8,128)}) %tuple.11, (s32[128]{0:T(128)}, s32[128]{0:T(128)}, f32[16,128,1024]{2,1,0:T(8,128)}, s32[128,1024]{1,0:T(8,128)}) %tuple.11), branch_computations={%region_2.3_spmd, %region_3.4_spmd} | conditional | bytes 8 | solution.py:483
  2.1 185.7 %branch_1_fun.1 = f32[16,128,1024]{2,1,0:T(8,128)S(1)} custom-call(s32[128]{0:T(128)} %get-tuple-element.28.offsets, s32[128]{0:T(128)} %get-tuple-element.29.widths, f32[16,128,1024]{2,1,0:T(8,128)} %get-tuple-element.30.x, s32[128,1024]{1,0:T(8,128)} %get-tuple-element.31.edge), custom_call_target="tpu_custom_call" | custom-call | tf_op jit(solution)/shard_map/cond/branch_1_fun/pallas_call | solution.py:483
  187.8 3.4 %copy.10 = f32[16,128,1024]{2,1,0:T(8,128)} copy(f32[16,128,1024]{2,1,0:T(8,128)S(1)} %get-tuple-element.32) | data formatting | bytes 16777216

commit v4 on v3

--- a/solution.py
+++ b/solution.py
@@ -415,6 +415,24 @@
             sent(c)
         for m in mates:
             out_copy(c, m).wait_recv()
+
+
+def decide(group, block, room, offsets, over):
+    shape = (group, offsets.shape[1])
+    rows = shape[1] // group
+    slot = lax.broadcasted_iota(jnp.int32, shape, 1) - rows * lax.broadcasted_iota(jnp.int32, shape, 0)
+    most = 0.0
+    for n in lengths(offsets[...], block):
+        n = jnp.broadcast_to(n.astype(jnp.float32), shape)
+        most = jnp.maximum(most, jnp.sum(jnp.where((slot >= 0) & (slot < rows), n, 0.0), 1, keepdims=True))
+    over[0] = (jnp.max(most) > room).astype(jnp.int32)
+
+
+def choose(index, branches, *operands):
+    traced = jax.make_jaxpr(lambda i, *args: lax.switch(i, branches, *args))(index, *operands)
+    (switch,) = [eqn for eqn in traced.eqns if eqn.primitive.name == "cond"]
+    assert list(switch.invars[1:]) == list(traced.jaxpr.invars[1:]) and not traced.consts
+    return switch.primitive.bind(index, *operands, **switch.params)[0]
 
 
 def body(frames, depth_offset, band_width, edge_level):
@@ -476,13 +494,14 @@
 
     whole = rows * spans
     half = whole // 2
-    up, down = lengths(depth_offset, block)
-    mine = jnp.arange(all_rows)[None] // rows == jnp.arange(group)[:, None]
-    taken = jnp.sum(jnp.where(mine, up + down * (2 * whole), 0), 1)
-    fits = jnp.max(jnp.maximum(lax.rem(taken, 2 * whole), lax.div(taken, 2 * whole))) <= half
-    return lax.cond(
-        fits, with_room(half, 0), with_room(whole, 1), depth_offset, band_width, frames, edge_level
-    )
+    over = pl.pallas_call(
+        functools.partial(decide, group, block, half),
+        out_shape=pltpu.SMEM((1,), jnp.int32),
+        in_specs=[pl.BlockSpec(memory_space=pltpu.VMEM)],
+        out_specs=pl.BlockSpec(memory_space=pltpu.SMEM),
+    )(depth_offset[None])
+    kernels = [with_room(half, 0), with_room(whole, 1)]
+    return choose(over.reshape(()), kernels, depth_offset, band_width, frames, edge_level)
 
 
 def solution(mesh):

time: 193 us -> 192 us (level)
    pallas_call x1 -> x2, Pallas kernels: 186 us -> 186 us  [the longest x1 186 us: choose(): return switch.primitive.bind(index, *operands, **switch.params)[0]]
where the time goes in v4:
time: 192 us; the launch traced here: 190 us
  Pallas kernels  186 us (97%)
  local copies, waits for them, and re-layouts  3.4 us (2%)
    pallas_call x1, Pallas kernels, choose(): return switch.primitive.bind(index, *operands, **switch.params)[0]  186 us

profile of v4, /device:TPU:26, one launch (start us, length us, event | category | flops | bytes accessed | tf_op | source)
XLA Modules:
  0.0 189.9 jit_solution(10773391766904285658)
XLA Ops:
  0.0 0.8 shard_map.54
  0.8 185.7 %conditional.1 = (f32[16,128,1024]{2,1,0:T(8,128)S(1)}) conditional(s32[]{:T(128)S(4)} %bitcast.1, (s32[128]{0:T(128)}, s32[128]{0:T(128)}, f32[16,128,1024]{2,1,0:T(8,128)}, s32[128,1024]{1,0:T(8,128)}) %tuple.11, (s32[128]{0:T(128)}, s32[128]{0:T(128)}, f32[16,128,1024]{2,1,0:T(8,128)}, s32[128,1024]{1,0:T(8,128)}) %tuple.11), branch_computations={%region_0.0_spmd, %region_1.0_spmd} | conditional | bytes 8 | solution.py:435
  0.8 185.7 %branch_0_fun.1 = f32[16,128,1024]{2,1,0:T(8,128)S(1)} custom-call(s32[128]{0:T(128)} %get-tuple-element.24.offsets, s32[128]{0:T(128)} %get-tuple-element.39.widths, f32[16,128,1024]{2,1,0:T(8,128)} %get-tuple-element.41.x, s32[128,1024]{1,0:T(8,128)} %get-tuple-element.43.edge), custom_call_target="tpu_custom_call" | custom-call | tf_op jit(solution)/shard_map/cond/branch_0_fun/pallas_call | solution.py:435
  186.5 3.4 %copy.16 = f32[16,128,1024]{2,1,0:T(8,128)} copy(f32[16,128,1024]{2,1,0:T(8,128)S(1)} %get-tuple-element.32) | data formatting | bytes 16777216

commit v5 on v4

--- a/solution.py
+++ b/solution.py
@@ -17,6 +17,7 @@
 LEAD = 4
 LAG = 1
 SLOTS = 3
+BUFFERS = 2
 UNROLL = 4
 LO = DIFFUSE + BAND - 1
 MESH = pl.DeviceIdType.MESH
@@ -34,6 +35,15 @@
     up = (jnp.maximum(offset, 0) + ROWS - 1) // ROWS
     down = (jnp.maximum(beyond, 0) + ROWS - 1) // ROWS
     return up, down
+
+
+def out_parts(chunks):
+    parts, c = [], 0
+    while c < chunks:
+        wide = 2 if c + 2 <= chunks - 2 else 1
+        parts.append((c, wide))
+        c += wide
+    return parts
 
 
 def sweep_pass(load, store, n_in, n_out, sweeps, streams):
@@ -91,12 +101,14 @@
     z = lax.div(me, group)
     tile_count = rows // ROWS
     pair = 2 if tile_count % 2 == 0 else 1
+    outs = out_parts(chunks)
+    buffer_of = [u for u, part in enumerate(outs) for _ in range(part[1])]
 
     def rows_of(j):
         return pl.ds(pl.multiple_of(j * rows, ROWS), rows)
 
-    def cols_of(c):
-        return pl.ds(c * LANES, LANES)
+    def cols_of(c, wide=1):
+        return pl.ds(c * LANES, wide * LANES)
 
     mates = sorted(range(1, group), key=lambda m: -m.bit_count())
 
@@ -147,22 +159,26 @@
             in_own.at[c],
         )
 
-    def out_copy(c, m):
+    def out_source(u, j):
+        c, wide = outs[u]
+        return made.at[u % BUFFERS, pl.ds(j * local, local), :, pl.ds(0, wide * LANES)]
+
+    def out_place(u):
+        c, wide = outs[u]
+        return out.at[:, rows_of(k), cols_of(c, wide)]
+
+    def out_copy(u, m):
         return pltpu.make_async_remote_copy(
-            src_ref=made.at[c % SLOTS, pl.ds(partner(m) * local, local)],
-            dst_ref=out.at[:, rows_of(k), cols_of(c)],
-            send_sem=out_send.at[c, m - 1],
-            recv_sem=out_recv.at[c, m - 1],
+            src_ref=out_source(u, partner(m)),
+            dst_ref=out_place(u),
+            send_sem=out_send.at[u, m - 1],
+            recv_sem=out_recv.at[u, m - 1],
             device_id={"scan": mate(m)},
             device_id_type=MESH,
         )
 
-    def out_local(c):
-        return pltpu.make_async_copy(
-            made.at[c % SLOTS, pl.ds(k * local, local)],
-            out.at[:, rows_of(k), cols_of(c)],
-            out_own.at[c],
-        )
+    def out_local(u):
+        return pltpu.make_async_copy(out_source(u, k), out_place(u), out_own.at[u])
 
     def z_copy(src, dst, sems, c, i, step):
         send, recv = sems
@@ -332,6 +348,7 @@
         lax.fori_loop(0, rows, one, 0)
 
     def depth(c):
+        u = buffer_of[c]
         win = wins[c % SLOTS]
         wait_recv(far_copies(c))
         pl.when(gets[1])(lambda: unpack(win, from_up[c], base_up, 0))
@@ -377,22 +394,23 @@
                 return prof[pl.ds(pl.multiple_of(t * rows + (p * pair + s) * ROWS, ROWS), ROWS), :]
 
             def store(t, s, value):
-                made[c % SLOTS, t, tiles[s], :] = value * scales[s]
+                made[u % BUFFERS, t, tiles[s], pl.ds((c - outs[u][0]) * LANES, LANES)] = value * scales[s]
 
             sweep_pass(load, store, block + 2 * DIFFUSE, block, DIFFUSE, pair)
             return 0
 
-        if c >= SLOTS:
-            sent(c - SLOTS)
+        if c == outs[u][0] and u >= BUFFERS:
+            sent(u - BUFFERS)
         lax.fori_loop(0, tile_count // pair, one, 0)
+        if c + 1 == sum(outs[u]):
+            for m in mates:
+                out_copy(u, m).start()
+            out_local(u).start()
+
+    def sent(u):
+        out_local(u).wait()
         for m in mates:
-            out_copy(c, m).start()
-        out_local(c).start()
-
-    def sent(c):
-        out_local(c).wait()
-        for m in mates:
-            out_copy(c, m).wait_send()
+            out_copy(u, m).wait_send()
 
     arrive(0)
     for c in range(chunks):
@@ -411,10 +429,11 @@
         wait_send(halo_copies(c))
         if c >= chunks - SLOTS:
             wait_send(far_copies(c))
-        if c >= chunks - SLOTS:
-            sent(c)
+    for u in range(len(outs)):
+        if u >= len(outs) - BUFFERS:
+            sent(u)
         for m in mates:
-            out_copy(c, m).wait_recv()
+            out_copy(u, m).wait_recv()
 
 
 def decide(group, block, room, offsets, over):
@@ -441,6 +460,7 @@
     chunks, rows, block = cols // LANES, all_rows // group, local * group
     hi, spans = after(block), block // ROWS
     bins = -(-(block + 2 * DIFFUSE) // ROWS) * ROWS
+    n_out = len(out_parts(chunks))
     dma = pltpu.SemaphoreType.DMA
     anywhere = pl.BlockSpec(memory_space=pl.ANY)
 
@@ -462,7 +482,7 @@
             + [vmem((3 * block + LO + hi) * rows, LANES)] * SLOTS
             + [
                 vmem(chunks, LO + block + hi + 2 * SWEEPS, rows, LANES),
-                vmem(SLOTS, block, rows, LANES),
+                vmem(BUFFERS, block, rows, 2 * LANES),
                 vmem(bins * rows, LANES),
                 vmem(rows, LANES),
                 packed,
@@ -479,16 +499,16 @@
                 dma((chunks, 2)),
                 dma((chunks, 2)),
                 dma((chunks, 2)),
-                dma((chunks, group - 1)),
-                dma((chunks, group - 1)),
-                dma((chunks,)),
+                dma((n_out, group - 1)),
+                dma((n_out, group - 1)),
+                dma((n_out,)),
                 dma,
                 table(all_rows),
                 table(all_rows),
                 dma((2,)),
             ],
             compiler_params=pltpu.CompilerParams(
-                collective_id=call, has_side_effects=True, vmem_limit_bytes=52 * 1024 * 1024
+                collective_id=call, has_side_effects=True, vmem_limit_bytes=54 * 1024 * 1024
             ),
         )
 

time: 192 us -> 195 us (1.016)
  Pallas kernels: 186 us -> 189 us
    pallas_call x1, Pallas kernels: 186 us -> 188 us  [choose(): return switch.primitive.bind(index, *operands, **switch.params)[0]]
where the time goes in v5:
time: 195 us; the launch traced here: 192 us
  Pallas kernels  189 us (97%)
  local copies, waits for them, and re-layouts  3.4 us (2%)
    pallas_call x1, Pallas kernels, choose(): return switch.primitive.bind(index, *operands, **switch.params)[0]  188 us

profile of v5, /device:TPU:26, one launch (start us, length us, event | category | flops | bytes accessed | tf_op | source)
XLA Modules:
  0.0 192.0 jit_solution(8845764203793512138)
XLA Ops:
  0.0 0.8 shard_map.54
  0.8 187.8 %conditional.1 = (f32[16,128,1024]{2,1,0:T(8,128)S(1)}) conditional(s32[]{:T(128)S(4)} %bitcast.1, (s32[128]{0:T(128)}, s32[128]{0:T(128)}, f32[16,128,1024]{2,1,0:T(8,128)}, s32[128,1024]{1,0:T(8,128)}) %tuple.11, (s32[128]{0:T(128)}, s32[128]{0:T(128)}, f32[16,128,1024]{2,1,0:T(8,128)}, s32[128,1024]{1,0:T(8,128)}) %tuple.11), branch_computations={%region_0.0_spmd, %region_1.0_spmd} | conditional | bytes 8 | solution.py:454
  0.8 187.7 %branch_0_fun.1 = f32[16,128,1024]{2,1,0:T(8,128)S(1)} custom-call(s32[128]{0:T(128)} %get-tuple-element.24.offsets, s32[128]{0:T(128)} %get-tuple-element.39.widths, f32[16,128,1024]{2,1,0:T(8,128)} %get-tuple-element.41.x, s32[128,1024]{1,0:T(8,128)} %get-tuple-element.43.edge), custom_call_target="tpu_custom_call" | custom-call | tf_op jit(solution)/shard_map/cond/branch_0_fun/pallas_call | solution.py:454
  188.6 3.4 %copy.16 = f32[16,128,1024]{2,1,0:T(8,128)} copy(f32[16,128,1024]{2,1,0:T(8,128)S(1)} %get-tuple-element.32) | data formatting | bytes 16777216

commit v6 on v5

--- a/solution.py
+++ b/solution.py
@@ -17,7 +17,7 @@
 LEAD = 4
 LAG = 1
 SLOTS = 3
-BUFFERS = 2
+BUFFERS = 3
 UNROLL = 4
 LO = DIFFUSE + BAND - 1
 MESH = pl.DeviceIdType.MESH

time: 195 us -> 195 us (level)
  no operation moved by 1% of the time
where the time goes in v6:
time: 195 us; the launch traced here: 192 us
  Pallas kernels  189 us (97%)
  local copies, waits for them, and re-layouts  3.4 us (2%)
    pallas_call x1, Pallas kernels, choose(): return switch.primitive.bind(index, *operands, **switch.params)[0]  188 us

profile of v6, /device:TPU:26, one launch (start us, length us, event | category | flops | bytes accessed | tf_op | source)
XLA Modules:
  0.0 192.0 jit_solution(512690923035779012)
XLA Ops:
  0.0 0.8 shard_map.54
  0.8 187.8 %conditional.1 = (f32[16,128,1024]{2,1,0:T(8,128)S(1)}) conditional(s32[]{:T(128)S(4)} %bitcast.1, (s32[128]{0:T(128)}, s32[128]{0:T(128)}, f32[16,128,1024]{2,1,0:T(8,128)}, s32[128,1024]{1,0:T(8,128)}) %tuple.11, (s32[128]{0:T(128)}, s32[128]{0:T(128)}, f32[16,128,1024]{2,1,0:T(8,128)}, s32[128,1024]{1,0:T(8,128)}) %tuple.11), branch_computations={%region_0.0_spmd, %region_1.0_spmd} | conditional | bytes 8 | solution.py:454
  0.8 187.7 %branch_0_fun.1 = f32[16,128,1024]{2,1,0:T(8,128)S(1)} custom-call(s32[128]{0:T(128)} %get-tuple-element.24.offsets, s32[128]{0:T(128)} %get-tuple-element.39.widths, f32[16,128,1024]{2,1,0:T(8,128)} %get-tuple-element.41.x, s32[128,1024]{1,0:T(8,128)} %get-tuple-element.43.edge), custom_call_target="tpu_custom_call" | custom-call | tf_op jit(solution)/shard_map/cond/branch_0_fun/pallas_call | solution.py:454
  188.6 3.4 %copy.16 = f32[16,128,1024]{2,1,0:T(8,128)} copy(f32[16,128,1024]{2,1,0:T(8,128)S(1)} %get-tuple-element.32) | data formatting | bytes 16777216

commit v7 on v4

--- a/solution.py
+++ b/solution.py
@@ -17,7 +17,7 @@
 LEAD = 4
 LAG = 1
 SLOTS = 3
-UNROLL = 4
+UNROLL = 8
 LO = DIFFUSE + BAND - 1
 MESH = pl.DeviceIdType.MESH
 RATE = 1.0 / STEP_SIZE

time: 192 us -> 192 us (level)
  no operation moved by 1% of the time
where the time goes in v7:
time: 192 us; the launch traced here: 190 us
  Pallas kernels  186 us (97%)
  local copies, waits for them, and re-layouts  3.4 us (2%)
    pallas_call x1, Pallas kernels, choose(): return switch.primitive.bind(index, *operands, **switch.params)[0]  186 us

profile of v7, /device:TPU:26, one launch (start us, length us, event | category | flops | bytes accessed | tf_op | source)
XLA Modules:
  0.0 189.9 jit_solution(4992153138025294867)
XLA Ops:
  0.0 0.8 shard_map.54
  0.8 185.7 %conditional.1 = (f32[16,128,1024]{2,1,0:T(8,128)S(1)}) conditional(s32[]{:T(128)S(4)} %bitcast.1, (s32[128]{0:T(128)}, s32[128]{0:T(128)}, f32[16,128,1024]{2,1,0:T(8,128)}, s32[128,1024]{1,0:T(8,128)}) %tuple.11, (s32[128]{0:T(128)}, s32[128]{0:T(128)}, f32[16,128,1024]{2,1,0:T(8,128)}, s32[128,1024]{1,0:T(8,128)}) %tuple.11), branch_computations={%region_0.0_spmd, %region_1.0_spmd} | conditional | bytes 8 | solution.py:435
  0.8 185.7 %branch_0_fun.1 = f32[16,128,1024]{2,1,0:T(8,128)S(1)} custom-call(s32[128]{0:T(128)} %get-tuple-element.24.offsets, s32[128]{0:T(128)} %get-tuple-element.39.widths, f32[16,128,1024]{2,1,0:T(8,128)} %get-tuple-element.41.x, s32[128,1024]{1,0:T(8,128)} %get-tuple-element.43.edge), custom_call_target="tpu_custom_call" | custom-call | tf_op jit(solution)/shard_map/cond/branch_0_fun/pallas_call | solution.py:435
  186.5 3.4 %copy.16 = f32[16,128,1024]{2,1,0:T(8,128)} copy(f32[16,128,1024]{2,1,0:T(8,128)S(1)} %get-tuple-element.32) | data formatting | bytes 16777216
